TPU v7x, 32 devices: a whole 2x2x4 slice. The times are simulated.
32 devices in a mesh: grp: 2 (over x), tp: 8 (over z, y), role: 2 (over core).
Axes of the slice: x: 2, y: 2, z: 4, core: 2. Of those that a mesh axis runs over, the one named last changes fastest.
Arguments:
- prompt_states: bfloat16 [2048, 8192], P(('grp', 'role'), 'tp'), parts along dimension 0, may hold values from -80 to 80
- kv_weight: bfloat16 [8192, 2048], P('tp'), may hold values from -0.0625 to 0.0625
- prompt_segments: int32 [4, 512], P(('grp', 'role')), parts along dimension 0, may hold values from 0 to 7, never falling along the last dimension, each value on 1 to 128 neighbouring positions
- page_dest: int32 [4, 4], P(('grp', 'role')), parts along dimension 0, may hold values from 0 to 7, as said below
- new_slot: int32 [4, 4], P(('grp', 'role')), parts along dimension 0, may hold values from 0 to 7, as said below
- cache_keys: bfloat16 [4, 64, 8, 128, 128], P(('grp', 'role'), 'tp'), parts along dimension 0, may hold values from -6 to 6
- cache_values: bfloat16 [4, 64, 8, 128, 128], P(('grp', 'role'), 'tp'), parts along dimension 0, may hold values from -6 to 6
- decode_queries: bfloat16 [4, 8, 8192], P(('grp', 'role')), parts along dimension 0, may hold values from -400 to 400
- request_pages: int32 [4, 8, 8], P(('grp', 'role')), parts along dimension 0, may hold values from 0 to 63, as said below
- context_lengths: int32 [4, 8], P(('grp', 'role')), parts along dimension 0, may hold values from 130 to 1024, as said below
- out_weight: bfloat16 [8192, 8192], P(None, 'tp'), may hold values from -1 to 1
Outputs:
- attention_out: bfloat16 [4, 8, 8192], P(('grp', 'role'), None, 'tp'), parts along dimension 0
There are 2 independent parts, one for each index of `grp`. A program takes and returns all parts, laid end to end along the dimension named above; an argument that names none is the same for every part. Nothing has to cross between parts.
Inputs may be any that keep to these rules, and one draw needn't show every extreme that they name: `page_dest`: no decode device receives more than 2 prompt pages; in each sub-replica some device receives exactly 2. `new_slot`: prompt pages that go to the same device have different slots. `request_pages`: in each sub-replica every pool page 0 to 63 appears exactly once among the 8 x 8 entries; every page that receives a prompt page stands at an entry below 1 of its list. `context_lengths`: in each sub-replica some request has exactly 1024 tokens.
All inputs are finite; a program needn't handle non-finite values.
Results may differ from a plain program's by a relative error of at most 0.024.
Values may be sent and summed in bfloat16 or wider, within the bound.
A program may use at most 128 MiB of HBM per device.

v0:
```python
import math

import jax
import jax.numpy as jnp
from jax import lax
from jax.sharding import PartitionSpec as P

KVH = 8
HD = 128


rope_base = 500000.0
neg_fill = -1e30


def rotate(key_heads, positions):
    half_width = key_heads.shape[-1] // 2
    frequency = rope_base ** (
        -(jnp.arange(half_width, dtype=jnp.float32) * 2.0) / key_heads.shape[-1]
    )
    angles = positions.astype(jnp.float32)[:, None] * frequency[None, :]
    cosine = jnp.cos(angles)[:, None, :]
    sine_part = jnp.sin(angles)[:, None, :]
    lower_half = key_heads[..., :half_width]
    upper_half = key_heads[..., half_width:]
    return jnp.concatenate(
        [
            lower_half * cosine - upper_half * sine_part,
            upper_half * cosine + lower_half * sine_part,
        ],
        axis=-1,
    )


def page_partials(owned_queries, key_pages, value_pages, page_limit):
    page_count, head_count, page_width, head_depth = key_pages.shape
    grouped = owned_queries.reshape(page_count, head_count, -1, head_depth)
    scores = jnp.einsum(
        "pgqd,pgtd->pgqt", grouped, key_pages, preferred_element_type=jnp.float32
    ) * (1.0 / math.sqrt(head_depth))
    is_live = jnp.arange(page_width)[None, None, None, :] < page_limit[:, None, None, None]
    page_max = jnp.max(jnp.where(is_live, scores, neg_fill), axis=-1)
    weights = jnp.exp(jnp.where(is_live, scores - page_max[..., None], neg_fill)).astype(
        jnp.bfloat16
    )
    page_sum = jnp.sum(weights.astype(jnp.float32), axis=-1)
    page_acc = jnp.einsum(
        "pgqt,pgtd->pgqd", weights, value_pages, preferred_element_type=jnp.float32
    )
    all_heads = head_count * grouped.shape[2]
    return (
        page_max.reshape(page_count, all_heads),
        page_sum.reshape(page_count, all_heads),
        page_acc.reshape(page_count, all_heads, head_depth),
    )


def fold_requests(owned_by, page_max, page_sum, page_acc):
    largest = jnp.max(jnp.where(owned_by[:, :, None], page_max[None], neg_fill), axis=1)
    factor = jnp.where(owned_by[:, :, None], jnp.exp(page_max[None] - largest[:, None, :]), 0.0)
    grand_sum = jnp.sum(factor * page_sum[None], axis=1)
    numerator = jnp.einsum("bsh,shd->bhd", factor, page_acc, precision=lax.Precision.HIGHEST)
    return (largest, grand_sum, numerator)


def finish(exchanged):
    maxima, partial_sums, partial_numer = exchanged
    largest = jnp.max(maxima, axis=0)
    factor = jnp.exp(maxima - largest[None])
    grand_sum = jnp.sum(factor * partial_sums, axis=0)
    summed = jnp.sum(factor[..., None] * partial_numer, axis=0)
    return (summed / grand_sum[..., None]).astype(jnp.bfloat16).reshape(summed.shape[0], -1)


def local(
    prompt_states,
    kv_weight,
    prompt_segments,
    page_dest,
    new_slot,
    cache_keys,
    cache_values,
    decode_queries,
    request_pages,
    context_lengths,
    out_weight,
):
    rank_count = lax.axis_size("tp")
    my_rank = lax.axis_index("tp")
    tokens = prompt_states.shape[0]
    share_len = tokens // rank_count
    kv_sum = lax.psum_scatter(
        jnp.dot(prompt_states, kv_weight, preferred_element_type=jnp.float32).astype(jnp.bfloat16),
        "tp",
        scatter_dimension=0,
        tiled=True,
    ).astype(jnp.float32)
    segments = prompt_segments[0]
    own_segments = lax.dynamic_slice_in_dim(segments, my_rank * share_len, share_len)
    token_index = my_rank * share_len + jnp.arange(share_len, dtype=jnp.int32)
    earlier = (segments[None, :] == own_segments[:, None]) & (
        jnp.arange(tokens, dtype=jnp.int32)[None, :] < token_index[:, None]
    )
    positions = jnp.sum(earlier.astype(jnp.int32), axis=1)
    kv_sum = kv_sum.reshape(share_len, 2, KVH, HD)
    new_keys = rotate(kv_sum[:, 0], positions).astype(jnp.bfloat16)
    new_values = kv_sum[:, 1].astype(jnp.bfloat16)
    fresh = jnp.stack([new_keys, new_values], axis=1).reshape(share_len, 2 * KVH * HD)
    page_owner = page_dest[0]
    page_count = page_owner.shape[0]
    arrived = lax.all_gather(fresh, "tp", axis=0, tiled=True)
    arrived = arrived.reshape(page_count, -1)
    pool_keys = cache_keys[0]
    pool_values = cache_values[0]
    pool_len = pool_keys.shape[0]
    page_width = pool_keys.shape[2]
    lands = (page_owner[None, :] == my_rank) & (
        new_slot[0][None, :] == jnp.arange(pool_len, dtype=jnp.int32)[:, None]
    )
    filled = jnp.any(lands, axis=1)
    incoming = jnp.dot(
        lands.astype(jnp.bfloat16), arrived, preferred_element_type=jnp.float32
    ).astype(jnp.bfloat16)
    incoming = incoming.reshape(pool_len, page_width, 2, KVH, HD)
    incoming_keys = incoming[:, :, 0].transpose(0, 2, 1, 3)
    incoming_values = incoming[:, :, 1].transpose(0, 2, 1, 3)
    slot_ids = my_rank * pool_len + jnp.arange(pool_len, dtype=jnp.int32)
    page_lists = request_pages[0]
    lengths = context_lengths[0]
    longest = page_lists.shape[1]
    matches = page_lists[:, :, None] == slot_ids[None, None, :]
    limits = lengths[:, None] - jnp.arange(longest, dtype=jnp.int32)[None, :] * page_width
    slot_limit = jnp.sum(jnp.where(matches, limits[:, :, None], 0), axis=(0, 1))
    owned_by = jnp.any(matches, axis=1)
    queries = decode_queries[0]
    owned_queries = jnp.dot(
        owned_by.T.astype(jnp.bfloat16), queries, preferred_element_type=jnp.float32
    ).astype(jnp.bfloat16)
    pool_keys = jnp.where(filled[:, None, None, None], incoming_keys, pool_keys)
    pool_values = jnp.where(filled[:, None, None, None], incoming_values, pool_values)
    page_max, page_sum, page_acc = page_partials(owned_queries, pool_keys, pool_values, slot_limit)
    largest, grand_sum, numerator = fold_requests(owned_by, page_max, page_sum, page_acc)
    head_part = finish(
        (
            lax.all_to_all(largest[None], "tp", split_axis=2, concat_axis=0, tiled=True),
            lax.all_to_all(grand_sum[None], "tp", split_axis=2, concat_axis=0, tiled=True),
            lax.all_to_all(numerator[None], "tp", split_axis=2, concat_axis=0, tiled=True),
        )
    )
    attention = lax.all_gather(head_part, "tp", axis=1, tiled=True)
    result = jnp.dot(attention, out_weight, preferred_element_type=jnp.float32).astype(jnp.bfloat16)
    return result[None]


def solution(mesh):
    in_specs = (
        P(("grp", "role"), "tp"),
        P("tp", None),
        P(("grp", "role"), None),
        P(("grp", "role"), None),
        P(("grp", "role"), None),
        P(("grp", "role"), "tp", None, None, None),
        P(("grp", "role"), "tp", None, None, None),
        P(("grp", "role"), None, None),
        P(("grp", "role"), None, None),
        P(("grp", "role"), None),
        P(None, "tp"),
    )
    out_specs = P(("grp", "role"), None, "tp")
    return jax.shard_map(local, mesh=mesh, in_specs=in_specs, out_specs=out_specs, check_vma=False)
```

profile of v0, /device:TPU:0, one launch (start us, length us, event | category | flops | bytes accessed | tf_op | source)
XLA Modules:
  0.0 226.3 jit_solution(7144228228054998697)
XLA Ops:
  6.5 0.0 copy-start
  6.5 0.0 reduce-scatter.2.cloned.1.call-start
  6.5 1.2 copy-done
  7.8 5.9 %convolution_convert_fusion.2 = bf16[512,2048]{1,0:T(8,128)(2,1)} fusion(bf16[512,1024]{1,0:T(8,128)(2,1)S(1)} %copy-done, bf16[1024,2048]{1,0:T(8,128)(2,1)} %param.12), kind=kOutput, calls=%fused_computation.2 | convolution fusion | flops 2148532224 | bytes 7340032 | tf_op jit(solution)/shard_map/dot_general | solution.py:93
  13.6 0.0 copy-start.4
  13.6 0.0 reduce-scatter.2.cloned.1.call-update
  13.7 0.0 copy-start.3
  13.7 0.0 copy-start.8
  13.7 0.0 copy-start.5
  13.7 0.0 copy-start.6
  13.7 0.0 copy-start.1
  13.7 0.0 all-gather.2.cloned.1.call-start
  13.8 0.5 copy-done.4
  14.3 0.1 dynamic-slice_bitcast_fusion
  14.4 0.2 convert_reduce_fusion.1
  14.6 0.2 multiply_cosine_fusion
  14.8 70.5 %reduce-scatter.2.cloned.1.call-done = bf16[64,2048]{1,0:T(8,128)(2,1)} async-done(((bf16[512,2048]{1,0:T(8,128)(2,1)}), bf16[64,2048]{1,0:T(8,128)(2,1)}) %reduce-scatter.2.cloned.1.call-update) | async-done | bytes 262160 | tf_op jit(solution)/shard_map/reduce_scatter | solution.py:92
  85.3 1.0 copy.42
  86.3 0.2 fusion.18
  86.5 0.1 pad_maximum_fusion
  86.6 0.8 copy.65
  87.4 0.0 all-gather.2.cloned.1.call-update
  87.5 0.0 copy-done.3
  87.5 0.1 compare_reduce_fusion
  87.6 0.0 copy-done.8
  87.6 0.0 copy-done.5
  87.6 0.6 fusion.32
  88.2 0.0 copy-done.6
  88.2 0.1 broadcast_subtract_fusion
  88.3 0.1 fusion.28
  88.4 0.1 iota_compare_fusion.1
  88.4 0.0 copy-done.1
  88.4 0.9 convolution_convert_fusion.1
  89.3 46.4 %all-gather.2.cloned.1.call-done = bf16[512,2048]{1,0:T(8,128)(2,1)} async-done(((bf16[64,2048]{1,0:T(8,128)(2,1)}), bf16[512,2048]{1,0:T(8,128)(2,1)}) %all-gather.2.cloned.1.call-update) | async-done | bytes 2097168 | tf_op jit(solution)/shard_map/all_gather | solution.py:111
  135.7 3.2 %reshape.198 = bf16[4,262144]{1,0:T(4,128)(2,1)S(1)} reshape(bf16[512,2048]{1,0:T(8,128)(2,1)} %all-gather.2.cloned.1.call-done) | data formatting | bytes 4194304 | tf_op jit(solution)/shard_map/reshape | solution.py:112
  138.9 1.9 convolution_convert_fusion
  140.8 0.0 copy-start.2
  140.8 0.0 copy-start.7
  140.8 0.0 copy-start.9
  140.8 1.0 fusion.37
  141.8 0.0 copy-done.2
  141.9 0.6 copy-done.7
  142.5 0.0 copy-done.9
  142.5 2.6 %select_reduce_fusion.1 = (f32[8,8,8]{2,1,0:T(8,128)S(1)}, f32[8,8,8,128]{3,2,1,0:T(8,128)S(1)}) fusion(pred[8,128]{1,0:T(8,128)(4,1)S(1)} %iota_compare_fusion.1, bf16[8,128,1,8,128]{4,0,3,2,1:T(8,128)(2,1)S(1)} %get-tuple-element.7, bf16[1,8,8,128,128]{4,3,2,1,0:T(8,128)(2,1)S(1)} %copy-done.7, pred[8]{0:T(512)(128)(4,1)S(1)} %copy-done.9, ...), kind=kOutput, calls=%fused_computation.27 | convolution fusion | flops 18021888 | bytes 4590600 | tf_op jit(solution)/shard_map/pgqd,pgtd->pgqt/dot_general | solution.py:38
  145.0 0.1 copy.37
  145.1 0.3 convert_reduce_fusion
  145.4 0.1 copy.38
  145.5 0.8 select_reduce_fusion
  146.2 1.6 multiply_reduce_fusion
  147.8 3.5 %all-to-all-start.2 = ((f32[1,8,64]{1,0,2:T(1,128)}), f32[1,8,64]{1,0,2:T(1,128)S(1)}, u32[]{:S(2)}, u32[]{:S(2)}) async-start(f32[1,8,64]{1,0,2:T(1,128)} %bitcast.34), calls=%async_computation.3 | async-start | bytes 65536 | tf_op jit(solution)/shard_map/all_to_all | solution.py:146
  151.3 4.7 %fusion.10 = f32[8,64,128]{2,1,0:T(8,128)} fusion(bf16[8,128,1,8,128]{4,0,3,2,1:T(8,128)(2,1)S(1)} %get-tuple-element.8, bf16[1,8,8,128,128]{4,3,2,1,0:T(8,128)(2,1)} %param.17, pred[8]{0:T(512)(128)(4,1)S(1)} %copy-done.9, f32[8,8,8,128]{3,2,1,0:T(8,128)S(1)} %get-tuple-element.16, f32[8,8,8]{2,1,0:T(8,128)S(1)} %get-tuple-element.15, ...), kind=kOutput, calls=%fused_computation.13 | convolution fusion | flops 18022400 | bytes 4721672 | tf_op jit(solution)/shard_map/pgqt,pgtd->pgqd/dot_general | solution.py:47
  156.1 1.7 all-to-all-done.2
  157.8 4.1 %all-to-all-start = ((f32[1,8,64]{1,0,2:T(1,128)}), f32[1,8,64]{1,0,2:T(1,128)S(1)}, u32[]{:S(2)}, u32[]{:S(2)}) async-start(f32[1,8,64]{1,0,2:T(1,128)} %bitcast.18), calls=%async_computation.1 | async-start | bytes 65536 | tf_op jit(solution)/shard_map/all_to_all | solution.py:145
  161.8 2.4 %convolution_bitcast_fusion = f32[1,8,64,128]{3,1,0,2:T(8,128)} fusion(f32[8,64,128]{2,1,0:T(8,128)} %fusion.10, f32[8,64]{0,1:T(8,128)} %select_reduce_fusion, f32[8,64]{0,1:T(8,128)S(1)} %bitcast.114, pred[8,8]{1,0:T(8,128)(4,1)S(1)} %compare_reduce_fusion), kind=kOutput, calls=%fused_computation.14 | convolution fusion | flops 6299648 | bytes 528448 | tf_op jit(solution)/shard_map/bsh,shd->bhd/dot_general | solution.py:62
  164.2 4.3 %all-to-all-done = f32[1,8,64]{1,0,2:T(1,128)S(1)} async-done(((f32[1,8,64]{1,0,2:T(1,128)}), f32[1,8,64]{1,0,2:T(1,128)S(1)}, u32[]{:S(2)}, u32[]{:S(2)}) %all-to-all-start) | async-done | bytes 2080 | tf_op jit(solution)/shard_map/all_to_all | solution.py:145
  168.5 3.4 %all-to-all-start.1 = ((f32[1,8,64,128]{3,1,0,2:T(8,128)}), f32[1,8,64,128]{3,1,0,2:T(8,128)S(1)}, u32[]{:S(2)}, u32[]{:S(2)}) async-start(f32[1,8,64,128]{3,1,0,2:T(8,128)} %convolution_bitcast_fusion), calls=%async_computation.2 | async-start | bytes 524288 | tf_op jit(solution)/shard_map/all_to_all | solution.py:147
  172.0 8.1 %all-to-all-done.1 = f32[1,8,64,128]{3,1,0,2:T(8,128)S(1)} async-done(((f32[1,8,64,128]{3,1,0,2:T(8,128)}), f32[1,8,64,128]{3,1,0,2:T(8,128)S(1)}, u32[]{:S(2)}, u32[]{:S(2)}) %all-to-all-start.1) | async-done | bytes 262176 | tf_op jit(solution)/shard_map/all_to_all | solution.py:147
  180.1 0.1 multiply_reduce_fusion.1
  180.2 0.1 fusion.29
  180.3 30.5 %all_gather.7 = bf16[8,8192]{1,0:T(8,128)(2,1)S(1)} all-gather(bf16[8,1024]{1,0:T(8,128)(2,1)S(1)} %fusion.29), channel_id=1, replica_groups=mesh['grp'=2,'tp'=8,'role'=2] {'tp'}, dimensions={1}, use_global_device_ids=true | all-gather | bytes 147456 | tf_op jit(solution)/shard_map/all_gather | solution.py:150
  210.8 8.7 %fusion.16 = bf16[1,8,1024]{2,1,0:T(8,128)(2,1)} fusion(bf16[8,8192]{1,0:T(8,128)(2,1)S(1)} %all_gather.7, bf16[8192,1024]{1,0:T(8,128)(2,1)} %param.21), kind=kOutput, calls=%fused_computation.17 | convolution fusion | flops 134225920 | bytes 16924672 | tf_op jit(solution)/shard_map/dot_general | solution.py:151
  (9 shorter events, 0.1 us)
Async XLA Ops:
  6.5 1.2 copy-start
  6.5 78.8 %reduce-scatter.2.cloned.1.call-start = ((), (), s32[]{:S(2)}) async-start(), calls=%async_computation.4 | async-start | bytes 2359296 | tf_op jit(solution)/shard_map/reduce_scatter | solution.py:92
  13.6 0.7 copy-start.4
  13.7 73.8 %copy-start.3 = (s32[1,8,8]{2,1,0:T(8,128)S(1)}, s32[1,8,8]{2,1,0:T(8,128)}, u32[]{:S(2)}) copy-start(s32[1,8,8]{2,1,0:T(8,128)} %param.19) | copy-start | bytes 772
  13.7 73.9 %copy-start.8 = (s32[1,4]{1,0:T(1,128)S(1)}, s32[1,4]{1,0:T(1,128)}, u32[]{:S(2)}) copy-start(s32[1,4]{1,0:T(1,128)} %param.14) | copy-start | bytes 52
  13.7 73.9 %copy-start.5 = (s32[1,4]{1,0:T(1,128)S(1)}, s32[1,4]{1,0:T(1,128)}, u32[]{:S(2)}) copy-start(s32[1,4]{1,0:T(1,128)} %param.15) | copy-start | bytes 52
  13.7 74.5 %copy-start.6 = (s32[1,8]{1,0:T(1,128)S(1)}, s32[1,8]{1,0:T(1,128)}, u32[]{:S(2)}) copy-start(s32[1,8]{1,0:T(1,128)} %param.20) | copy-start | bytes 100
  13.7 74.7 %copy-start.1 = (bf16[1,8,8192]{2,1,0:T(8,128)(2,1)S(1)}, bf16[1,8,8192]{2,1,0:T(8,128)(2,1)}, u32[]{:S(2)}) copy-start(bf16[1,8,8192]{2,1,0:T(8,128)(2,1)} %param.18) | copy-start | bytes 393220
  13.7 122.0 %all-gather.2.cloned.1.call-start = ((), (), s32[]{:S(2)}) async-start(), calls=%async_computation.5 | async-start | bytes 2359296 | tf_op jit(solution)/shard_map/all_gather | solution.py:111
  140.8 1.0 copy-start.2
  140.8 1.7 copy-start.7
  140.8 1.7 copy-start.9
  147.8 10.0 %all-to-all-start.2 = ((f32[1,8,64]{1,0,2:T(1,128)}), f32[1,8,64]{1,0,2:T(1,128)S(1)}, u32[]{:S(2)}, u32[]{:S(2)}) async-start(f32[1,8,64]{1,0,2:T(1,128)} %bitcast.34), calls=%async_computation.3 | async-start | bytes 65536 | tf_op jit(solution)/shard_map/all_to_all | solution.py:146
  157.8 10.7 %all-to-all-start = ((f32[1,8,64]{1,0,2:T(1,128)}), f32[1,8,64]{1,0,2:T(1,128)S(1)}, u32[]{:S(2)}, u32[]{:S(2)}) async-start(f32[1,8,64]{1,0,2:T(1,128)} %bitcast.18), calls=%async_computation.1 | async-start | bytes 65536 | tf_op jit(solution)/shard_map/all_to_all | solution.py:145
  168.5 11.6 %all-to-all-start.1 = ((f32[1,8,64,128]{3,1,0,2:T(8,128)}), f32[1,8,64,128]{3,1,0,2:T(8,128)S(1)}, u32[]{:S(2)}, u32[]{:S(2)}) async-start(f32[1,8,64,128]{3,1,0,2:T(8,128)} %convolution_bitcast_fusion), calls=%async_computation.2 | async-start | bytes 524288 | tf_op jit(solution)/shard_map/all_to_all | solution.py:147
Sparse Core Ops, SparseCore 0:
  13.8 71.4 reduce-scatter.1
  87.6 48.1 all-gather.1
where the time goes:
time: 227 us; the launch traced here: 226 us
  waiting for transfers between devices  131 us (58%)
  blocking collectives  30.5 us (13%)
  matrix products  27 us (12%)
  between operations  13.6 us (6%)
  starting transfers between devices  11 us (5%)
  local copies, waits for them, and re-layouts  8.64 us (4%)
  other arithmetic  4.53 us (2%)
    reduce_scatter x1, waiting for transfers between devices, local(): lax.psum_scatter(jnp.dot(prompt_states, kv_weight, preferred_element_type...  70.5 us
    all_gather x1, waiting for transfers between devices, local(): arrived = lax.all_gather(fresh, 'tp', axis=0, tiled=True)  46.4 us
    all_gather x1, blocking collectives, local(): attention = lax.all_gather(head_part, 'tp', axis=1, tiled=True)  30.5 us
    dot_general x1, matrix products, local(): jnp.dot(attention, out_weight, preferred_element_type=jnp.float32)  8.65 us
    all_to_all x1, waiting for transfers between devices, local(): lax.all_to_all(numerator[None], 'tp', split_axis=2, concat_axis=0, tiled=...  8.11 us
    dot_general x1, matrix products, local(): jnp.dot(prompt_states, kv_weight, preferred_element_type=jnp.float32)  5.88 us
    dot_general x1, matrix products, page_partials(): jnp.einsum('pgqt,pgtd->pgqd', weights, value_pages, preferred_element_typ...  4.74 us
  transfers between devices with their start and end apart: 5, of which 5 were waited for; matrix products, arithmetic and copies ran while one was open for 4% of the time, Pallas kernels for 0%

commit v1 on v0

--- a/solution.py
+++ b/solution.py
@@ -1,8 +1,12 @@
+import functools
 import math
 
 import jax
 import jax.numpy as jnp
+import numpy as np
 from jax import lax
+from jax.experimental import pallas as pl
+from jax.experimental.pallas import tpu as pltpu
 from jax.sharding import PartitionSpec as P
 
 KVH = 8
@@ -11,6 +15,520 @@
 
 rope_base = 500000.0
 neg_fill = -1e30
+
+
+def cos_turn_coefficients():
+    nodes = 0.125 * (1.0 + np.cos((np.arange(400) + 0.5) * np.pi / 400))
+    basis = np.polynomial.chebyshev.Chebyshev.fit(
+        nodes, np.cos(2.0 * np.pi * np.sqrt(nodes)), 8, domain=[0.0, 0.25]
+    )
+    return [float(c) for c in basis.convert(kind=np.polynomial.Polynomial).coef]
+
+
+def rotation_tables(seg_row, tokens, width):
+    index = lax.broadcasted_iota(jnp.int32, (tokens, width), 0)
+    start = jnp.zeros((tokens, width), jnp.int32)
+    for value in range(1, 8):
+        first = jnp.sum((seg_row < value).astype(jnp.int32), axis=1, keepdims=True)
+        start = jnp.maximum(start, jnp.where(first <= index, first, 0))
+    position = (index - start).astype(jnp.float32)
+    lane = lax.broadcasted_iota(jnp.int32, (1, width), 1)
+    half = width // 2
+    low = lane < half
+    exponent = jnp.where(low, lane, lane - half).astype(jnp.float32) * (2.0 / width)
+    turns = jnp.exp(exponent * (-math.log(rope_base))) * (1.0 / (2.0 * math.pi))
+    phase = position * turns
+    phase = phase - jnp.round(phase)
+    phase = phase - jnp.where(low, 0.0, 0.25)
+    phase = phase - jnp.round(phase)
+    square = phase * phase
+    coefficients = cos_turn_coefficients()
+    value = jnp.full_like(square, coefficients[-1])
+    for c in coefficients[-2::-1]:
+        value = value * square + c
+    turned = pltpu.roll(value, half, 1)
+    return jnp.where(low, value, turned), jnp.where(low, turned, value)
+
+
+def fused_kernel(
+    ranks,
+    x_hbm,
+    w_hbm,
+    seg_ref,
+    dest_ref,
+    slot_ref,
+    kc_hbm,
+    vc_hbm,
+    q_ref,
+    rp_ref,
+    len_ref,
+    ow_hbm,
+    out_ref,
+    x_v,
+    wk_v,
+    wv_v,
+    kc_v,
+    vc_v,
+    ow_v,
+    v_new,
+    q_all,
+    qp,
+    cos_v,
+    sin_v,
+    live_v,
+    s_send,
+    s_recv,
+    w_all,
+    num_send,
+    num_recv,
+    stat_send,
+    stat_recv,
+    acc_send,
+    acc_recv,
+    att_all,
+    x_sem,
+    wk_sem,
+    wv_sem,
+    kc_sem,
+    vc_sem,
+    ow_sem,
+    tx,
+    rx,
+):
+    me = lax.axis_index("tp")
+    tokens, features = x_v.shape
+    pools = kc_hbm.shape[1]
+    pages = dest_ref.shape[1]
+    page = kc_hbm.shape[3]
+    requests = q_ref.shape[1]
+    group = q_ref.shape[2] // (KVH * HD)
+    rows = group * requests
+    chunk = ow_v.shape[1]
+    scale = 1.0 / math.sqrt(HD)
+    halves = KVH // 2
+
+    barrier = pltpu.get_barrier_semaphore()
+    for d in range(1, ranks):
+        pl.semaphore_signal(barrier, inc=1, device_id={"tp": lax.rem(me + d, ranks)})
+
+    def pair_of(i):
+        return lax.rem(me // 2 + 1 + i, halves)
+
+    def head_of(i):
+        return lax.rem(me + 1 + i, ranks)
+
+    def x_copy():
+        return pltpu.make_async_copy(x_hbm, x_v, x_sem)
+
+    def wk_copy(i):
+        return pltpu.make_async_copy(
+            w_hbm.at[:, pl.ds(pl.multiple_of(pair_of(i) * (2 * HD), 2 * HD), 2 * HD)],
+            wk_v.at[i],
+            wk_sem.at[i],
+        )
+
+    def wv_copy(i):
+        return pltpu.make_async_copy(
+            w_hbm.at[:, pl.ds(pl.multiple_of((halves + i) * (2 * HD), 2 * HD), 2 * HD)],
+            wv_v.at[i],
+            wv_sem.at[i],
+        )
+
+    def kc_copy(i):
+        return pltpu.make_async_copy(
+            kc_hbm.at[0, i], kc_v.at[:, pl.ds(i * page, page), :], kc_sem.at[i]
+        )
+
+    def vc_copy(i):
+        return pltpu.make_async_copy(
+            vc_hbm.at[0, i], vc_v.at[:, pl.ds(i * page, page), :], vc_sem.at[i]
+        )
+
+    def ow_copy(i):
+        return pltpu.make_async_copy(
+            ow_hbm.at[pl.ds(i * chunk, chunk), :], ow_v.at[i], ow_sem.at[i]
+        )
+
+    x_copy().start()
+    for i in range(halves):
+        wk_copy(i).start()
+    for i in range(halves):
+        wv_copy(i).start()
+    for i in range(pools):
+        kc_copy(i).start()
+    for i in range(pools):
+        vc_copy(i).start()
+
+    def remote(kind, src, dst, peer):
+        return pltpu.make_async_remote_copy(
+            src_ref=src,
+            dst_ref=dst,
+            send_sem=tx.at[kind, peer],
+            recv_sem=rx.at[kind, me],
+            device_id={"tp": peer},
+        )
+
+    def score_send(peer):
+        return remote(0, s_send.at[peer], s_recv.at[me], peer)
+
+    def weight_send(peer):
+        return remote(1, w_all.at[me], w_all.at[me], peer)
+
+    def num_copy(peer):
+        return remote(2, num_send.at[peer], num_recv.at[me], peer)
+
+    def stat_copy(peer):
+        return remote(3, stat_send.at[peer], stat_recv.at[me], peer)
+
+    def acc_copy(peer):
+        return remote(4, acc_send.at[peer], acc_recv.at[me], peer)
+
+    def att_copy(peer):
+        return remote(5, att_all.at[me], att_all.at[me], peer)
+
+    def arrival(kind, ref, source):
+        pltpu.make_async_remote_copy(
+            src_ref=ref.at[source],
+            dst_ref=ref.at[source],
+            send_sem=tx.at[kind, source],
+            recv_sem=rx.at[kind, source],
+            device_id={"tp": source},
+        ).wait_recv()
+
+    lists = rp_ref[0]
+    longest = lists.shape[1]
+    entry = lax.broadcasted_iota(jnp.int32, (requests, longest), 1)
+    request = lax.broadcasted_iota(jnp.int32, (requests, longest), 0)
+    length = jnp.zeros((requests, longest), jnp.int32)
+    for r in range(requests):
+        length = jnp.where(request == r, len_ref[0, r], length)
+    limit = length - entry * page
+
+    targets = [dest_ref[0, p] * pools + slot_ref[0, p] for p in range(pages)]
+    token = lax.broadcasted_iota(jnp.int32, (requests, page), 1)
+    for s in range(pools):
+        g = me * pools + s
+        kept = jnp.int32(1)
+        for p in range(pages):
+            kept = jnp.where(targets[p] == g, 0, kept)
+        bound = jnp.sum(jnp.where(lists == g, limit * kept, 0), axis=1, keepdims=True)
+        live_v[:, s * page : (s + 1) * page] = jnp.where(token < bound, 1.0, 0.0)
+    owners, bounds = [], []
+    for p in range(pages):
+        hit = lists == targets[p]
+        owners.append(jnp.sum(jnp.where(hit, request, 0), keepdims=True))
+        bounds.append(jnp.sum(jnp.where(hit, limit, 0), keepdims=True))
+
+    q_rows = q_ref[0].astype(jnp.float32)
+    lane = lax.broadcasted_iota(jnp.int32, (1, HD), 1)
+    sign = jnp.where(lane < HD // 2, 1.0, -1.0)
+    pick_row = lax.broadcasted_iota(jnp.int32, (pages * group, rows), 0)
+    pick_col = lax.broadcasted_iota(jnp.int32, (pages * group, rows), 1)
+    owner_rows = jnp.zeros((pages * group, rows), jnp.int32)
+    for p in range(pages):
+        owner_rows = jnp.where(pick_row // group == p, owners[p], owner_rows)
+    pick = jnp.where(pick_col == (pick_row % group) * requests + owner_rows, 1.0, 0.0).astype(
+        jnp.bfloat16
+    )
+    for h in range(KVH):
+        part = jnp.concatenate(
+            [
+                q_rows[:, (h * group + k) * HD : (h * group + k + 1) * HD]
+                for k in range(group)
+            ],
+            axis=0,
+        )
+        both = jnp.concatenate([part, pltpu.roll(part, HD // 2, 1) * sign], axis=1).astype(
+            jnp.bfloat16
+        )
+        q_all[h] = both
+        qp[h] = jnp.dot(pick, both, preferred_element_type=jnp.float32).astype(jnp.bfloat16)
+
+    cosine, sine = rotation_tables(seg_ref[...], tokens, HD)
+    cos_v[...] = cosine
+    sin_v[...] = sine
+
+    pl.semaphore_wait(barrier, ranks - 1)
+    x_copy().wait()
+
+    @pl.loop(0, halves)
+    def _(i):
+        wk_copy(i).wait()
+        product = jnp.dot(x_v[...], wk_v[i], preferred_element_type=jnp.float32)
+        for j in range(2):
+            h = pair_of(i) * 2 + j
+            keys = product[:, j * HD : (j + 1) * HD]
+            turned = jnp.concatenate([keys * cos_v[...], keys * sin_v[...]], axis=1).astype(
+                jnp.bfloat16
+            )
+            scores = lax.dot_general(
+                qp[h], turned, (((1,), (1,)), ((), ())), preferred_element_type=jnp.float32
+            )
+            for p in range(pages):
+                s_send[h, :, p * page : (p + 1) * page] = (
+                    scores[p * group : (p + 1) * group, p * page : (p + 1) * page] * scale
+                )
+
+            @pl.when(h != me)
+            def _():
+                score_send(h).start()
+
+    for i in range(ranks):
+        ow_copy(i).start()
+
+    @pl.loop(0, halves)
+    def _(i):
+        wv_copy(i).wait()
+        product = jnp.dot(x_v[...], wv_v[i], preferred_element_type=jnp.float32)
+        for j in range(2):
+            v_new[i * 2 + j] = product[:, j * HD : (j + 1) * HD].astype(jnp.bfloat16)
+
+    total_scores = s_send[me]
+    for d in range(1, ranks):
+        source = lax.rem(me + d, ranks)
+        arrival(0, s_recv, source)
+        total_scores = total_scores + s_recv[source]
+    page_token = lax.broadcasted_iota(jnp.int32, (group, page), 1)
+    new_max, new_sum = [], []
+    for p in range(pages):
+        alive = page_token < bounds[p]
+        scores = total_scores[:, p * page : (p + 1) * page]
+        top = jnp.max(jnp.where(alive, scores, neg_fill), axis=1, keepdims=True)
+        weight = jnp.exp(jnp.where(alive, scores - top, neg_fill)).astype(jnp.bfloat16)
+        w_all[me, :, p * page : (p + 1) * page] = weight
+        new_max.append(top)
+        new_sum.append(jnp.sum(weight.astype(jnp.float32), axis=1, keepdims=True))
+    for d in range(1, ranks):
+        weight_send(lax.rem(me + d, ranks)).start()
+
+    for i in range(pools):
+        kc_copy(i).wait()
+    for i in range(pools):
+        vc_copy(i).wait()
+    stat_lane = lax.broadcasted_iota(jnp.int32, (rows, HD), 1)
+
+    def resident(i, stats):
+        h = head_of(i)
+        scores = (
+            lax.dot_general(
+                q_all[h][:, :HD],
+                kc_v[h],
+                (((1,), (1,)), ((), ())),
+                preferred_element_type=jnp.float32,
+            )
+            * scale
+        )
+        mask = jnp.concatenate([live_v[...]] * group, axis=0) > 0.5
+        top = jnp.max(jnp.where(mask, scores, neg_fill), axis=1, keepdims=True)
+        weight = jnp.where(mask, jnp.exp(jnp.where(mask, scores - top, 0.0)), 0.0).astype(
+            jnp.bfloat16
+        )
+        total = jnp.sum(weight.astype(jnp.float32), axis=1, keepdims=True)
+        num_send[h] = jnp.dot(weight, vc_v[h], preferred_element_type=jnp.float32).astype(
+            jnp.bfloat16
+        )
+
+        @pl.when(h != me)
+        def _():
+            num_copy(h).start()
+
+        stats = jnp.where(stat_lane == h, top, stats)
+        return jnp.where(stat_lane == h + KVH, total, stats)
+
+    stats = lax.fori_loop(0, KVH, resident, jnp.zeros((rows, HD), jnp.float32))
+    padded = jnp.concatenate([stats, jnp.zeros((HD - rows, HD), jnp.float32)], axis=0)
+    flipped = jnp.transpose(padded)
+    for h in range(KVH):
+        stat_send[h, 0:1, :] = flipped[h : h + 1, :]
+        stat_send[h, 1:2, :] = flipped[KVH + h : KVH + h + 1, :]
+    for d in range(1, ranks):
+        stat_copy(lax.rem(me + d, ranks)).start()
+
+    @pl.loop(0, ranks)
+    def _(i):
+        h = lax.rem(me + i, ranks)
+
+        @pl.when(h != me)
+        def _():
+            arrival(1, w_all, h)
+
+        weight = w_all[h]
+        values = v_new[h]
+        acc_send[h] = jnp.concatenate(
+            [
+                jnp.dot(
+                    weight[:, p * page : (p + 1) * page],
+                    values[p * page : (p + 1) * page],
+                    preferred_element_type=jnp.float32,
+                )
+                for p in range(pages)
+            ],
+            axis=0,
+        ).astype(jnp.bfloat16)
+
+        @pl.when(h != me)
+        def _():
+            acc_copy(h).start()
+
+    source_row = lax.broadcasted_iota(jnp.int32, (HD, HD), 0)
+    for d in range(1, ranks):
+        arrival(3, stat_recv, lax.rem(me + d, ranks))
+    maxima = jnp.zeros((HD, HD), jnp.float32)
+    for d in range(ranks):
+        block = stat_send[me] if d == 0 else stat_recv[lax.rem(me + d, ranks)]
+        maxima = jnp.where(source_row == d, block[0:1, :], maxima)
+        maxima = jnp.where(source_row == d + ranks, block[1:2, :], maxima)
+    columns = jnp.transpose(maxima)[:rows]
+    old_max = [columns[:, d : d + 1] for d in range(ranks)]
+    old_sum = [columns[:, ranks + d : ranks + d + 1] for d in range(ranks)]
+    row_request = lax.broadcasted_iota(jnp.int32, (rows, HD), 0) % requests
+
+    def spread(value):
+        wide = jnp.broadcast_to(value, (group, HD))
+        return jnp.broadcast_to(wide[:, None, :], (group, requests, HD)).reshape(rows, HD)
+
+    mine = [row_request == owners[p] for p in range(pages)]
+    fresh_max = [jnp.where(mine[p], spread(new_max[p]), neg_fill) for p in range(pages)]
+    top = fresh_max[0]
+    for value in fresh_max[1:] + old_max:
+        top = jnp.maximum(top, value)
+    total = jnp.zeros((rows, HD), jnp.float32)
+    numer = jnp.zeros((rows, HD), jnp.float32)
+    for d in range(ranks):
+        source = lax.rem(me + d, ranks)
+        if d:
+            arrival(2, num_recv, source)
+        factor = jnp.exp(old_max[d] - top)
+        total = total + factor * old_sum[d]
+        block = num_send[me] if d == 0 else num_recv[source]
+        numer = numer + factor * block.astype(jnp.float32)
+    fresh_factor = [
+        jnp.where(mine[p], jnp.exp(fresh_max[p] - top), 0.0) for p in range(pages)
+    ]
+    for p in range(pages):
+        total = total + fresh_factor[p] * spread(new_sum[p])
+    fresh_acc = acc_send[me].astype(jnp.float32)
+    for d in range(1, ranks):
+        source = lax.rem(me + d, ranks)
+        arrival(4, acc_recv, source)
+        fresh_acc = fresh_acc + acc_recv[source].astype(jnp.float32)
+    for p in range(pages):
+        numer = numer + fresh_factor[p] * spread(fresh_acc[p * group : (p + 1) * group])
+    joined = (numer / total).astype(jnp.bfloat16)
+    for k in range(group):
+        att_all[me, :, k * HD : (k + 1) * HD] = joined[k * requests : (k + 1) * requests]
+    for d in range(1, ranks):
+        att_copy(lax.rem(me + d, ranks)).start()
+
+    for i in range(ranks):
+        ow_copy(i).wait()
+
+    def project(i, result):
+        source = lax.rem(me + i, ranks)
+
+        @pl.when(source != me)
+        def _():
+            arrival(5, att_all, source)
+
+        return result + jnp.dot(
+            att_all[source], ow_v[source], preferred_element_type=jnp.float32
+        )
+
+    result = lax.fori_loop(
+        0, ranks, project, jnp.zeros((requests, ow_v.shape[2]), jnp.float32)
+    )
+    out_ref[0] = result.astype(out_ref.dtype)
+
+    for d in range(1, ranks):
+        peer = lax.rem(me + d, ranks)
+        score_send(peer).wait_send()
+        weight_send(peer).wait_send()
+        num_copy(peer).wait_send()
+        stat_copy(peer).wait_send()
+        acc_copy(peer).wait_send()
+        att_copy(peer).wait_send()
+
+
+def fused(
+    prompt_states,
+    kv_weight,
+    prompt_segments,
+    page_dest,
+    new_slot,
+    cache_keys,
+    cache_values,
+    decode_queries,
+    request_pages,
+    context_lengths,
+    out_weight,
+):
+    ranks = lax.axis_size("tp")
+    tokens, features = prompt_states.shape
+    pools, page = cache_keys.shape[1], cache_keys.shape[3]
+    pages = page_dest.shape[1]
+    requests = decode_queries.shape[1]
+    group = decode_queries.shape[2] // (KVH * HD)
+    rows = group * requests
+    chunk = out_weight.shape[0] // ranks
+    width = out_weight.shape[1]
+    half = KVH // 2
+    vmem = pl.BlockSpec(memory_space=pltpu.VMEM)
+    smem = pl.BlockSpec(memory_space=pltpu.SMEM)
+    hbm = pl.BlockSpec(memory_space=pl.ANY)
+    bf16, f32 = jnp.bfloat16, jnp.float32
+    return pl.pallas_call(
+        functools.partial(fused_kernel, ranks),
+        out_shape=jax.ShapeDtypeStruct((1, requests, width), bf16),
+        in_specs=[hbm, hbm, vmem, smem, smem, hbm, hbm, vmem, vmem, smem, hbm],
+        out_specs=vmem,
+        scratch_shapes=[
+            pltpu.VMEM((tokens, features), bf16),
+            pltpu.VMEM((half, features, 2 * HD), bf16),
+            pltpu.VMEM((half, features, 2 * HD), bf16),
+            pltpu.VMEM((KVH, pools * page, HD), bf16),
+            pltpu.VMEM((KVH, pools * page, HD), bf16),
+            pltpu.VMEM((ranks, chunk, width), bf16),
+            pltpu.VMEM((KVH, tokens, HD), bf16),
+            pltpu.VMEM((KVH, rows, 2 * HD), bf16),
+            pltpu.VMEM((KVH, pages * group, 2 * HD), bf16),
+            pltpu.VMEM((tokens, HD), f32),
+            pltpu.VMEM((tokens, HD), f32),
+            pltpu.VMEM((requests, pools * page), f32),
+            pltpu.VMEM((ranks, group, tokens), f32),
+            pltpu.VMEM((ranks, group, tokens), f32),
+            pltpu.VMEM((ranks, group, tokens), bf16),
+            pltpu.VMEM((ranks, rows, HD), bf16),
+            pltpu.VMEM((ranks, rows, HD), bf16),
+            pltpu.VMEM((ranks, 8, HD), f32),
+            pltpu.VMEM((ranks, 8, HD), f32),
+            pltpu.VMEM((ranks, pages * group, HD), bf16),
+            pltpu.VMEM((ranks, pages * group, HD), bf16),
+            pltpu.VMEM((ranks, requests, chunk), bf16),
+            pltpu.SemaphoreType.DMA,
+            pltpu.SemaphoreType.DMA((half,)),
+            pltpu.SemaphoreType.DMA((half,)),
+            pltpu.SemaphoreType.DMA((pools,)),
+            pltpu.SemaphoreType.DMA((pools,)),
+            pltpu.SemaphoreType.DMA((ranks,)),
+            pltpu.SemaphoreType.DMA((6, ranks)),
+            pltpu.SemaphoreType.DMA((6, ranks)),
+        ],
+        compiler_params=pltpu.CompilerParams(
+            collective_id=0, has_side_effects=True, vmem_limit_bytes=60 * 1024 * 1024
+        ),
+    )(
+        prompt_states,
+        kv_weight,
+        prompt_segments,
+        page_dest,
+        new_slot,
+        cache_keys,
+        cache_values,
+        decode_queries,
+        request_pages,
+        context_lengths,
+        out_weight,
+    )
 
 
 def rotate(key_heads, positions):
@@ -167,4 +685,5 @@
         P(None, "tp"),
     )
     out_specs = P(("grp", "role"), None, "tp")
-    return jax.shard_map(local, mesh=mesh, in_specs=in_specs, out_specs=out_specs, check_vma=False)
+    step = fused if mesh.shape["tp"] == KVH else local
+    return jax.shard_map(step, mesh=mesh, in_specs=in_specs, out_specs=out_specs, check_vma=False)

time: 227 us -> 32.5 us (0.14)
  waiting for transfers between devices: 131 us -> 0 us
  Pallas kernels: 0 us -> 31 us
  blocking collectives: 30.5 us -> 0 us
  matrix products: 27 us -> 0 us
  between operations: 13.6 us -> 0.01 us
  starting transfers between devices: 11 us -> 0 us
  local copies, waits for them, and re-layouts: 8.64 us -> 1.32 us
  other arithmetic: 4.53 us -> 0 us
    reduce_scatter x1 -> x0, waiting for transfers between devices: 70.5 us -> none  [local(): lax.psum_scatter(jnp.dot(prompt_states, kv_weight, preferred_element_type...]
    all_gather x1 -> x0, waiting for transfers between devices: 46.4 us -> none  [local(): arrived = lax.all_gather(fresh, 'tp', axis=0, tiled=True)]
    pallas_call x0 -> x1, Pallas kernels: none -> 31 us  [fused(): pl.pallas_call(functools.partial(fused_kernel, ranks), out_shape=jax.Shap...]
    all_gather x1 -> x0, blocking collectives: 30.5 us -> none  [local(): attention = lax.all_gather(head_part, 'tp', axis=1, tiled=True)]
    dot_general x7 -> x0, matrix products: 27 us -> none  [the longest x1 8.65 us: local(): jnp.dot(attention, out_weight, preferred_element_type=jnp.float32)]
    all_to_all x3 -> x0, waiting for transfers between devices: 14.1 us -> none  [the longest x1 8.11 us: local(): lax.all_to_all(numerator[None], 'tp', split_axis=2, concat_axis=0, tiled=...]
    all_to_all x3 -> x0, starting transfers between devices: 11 us -> none  [the longest x1 4.05 us: local(): lax.all_to_all(largest[None], 'tp', split_axis=2, concat_axis=0, tiled=True)]
    reshape x1 -> x0, local copies, waits for them, and re-layouts: 3.21 us -> none  [local(): arrived = arrived.reshape(page_count, -1)]
  transfers between devices with their start and end apart: 5 -> 0, of which waited for: 5 -> 0; matrix products, arithmetic and copies ran while one was open for 4% -> 0% of each run, Pallas kernels for 0% -> 0%
where the time goes in v1:
time: 32.5 us; the launch traced here: 32.3 us
  Pallas kernels  31 us (95%)
  local copies, waits for them, and re-layouts  1.32 us (4%)
    pallas_call x1, Pallas kernels, fused(): pl.pallas_call(functools.partial(fused_kernel, ranks), out_shape=jax.Shap...  31 us
    unnamed x1, local copies, waits for them, and re-layouts  1.32 us

profile of v1, /device:TPU:0, one launch (start us, length us, event | category | flops | bytes accessed | tf_op | source)
XLA Modules:
  0.0 32.3 jit_solution(13611657619270904067)
XLA Ops:
  0.0 31.0 %shard_map.109 = bf16[1,8,1024]{2,1,0:T(8,128)(2,1)} custom-call(bf16[512,1024]{1,0:T(8,128)(2,1)} %x_hbm.1, bf16[1024,2048]{1,0:T(8,128)(2,1)} %w_hbm.1, s32[1,512]{1,0:T(1,128)} %seg_ref.1, s32[1,4]{1,0:T(1,128)} %dest_ref.1, s32[1,4]{1,0:T(1,128)} %slot_ref.1, bf16[1,8,8,128,128]{4,3,2,1,0:T(8,128)(2,1)} %kc_hbm.1, bf16[1,8,8,128,128]{4,3,2,1,0:T(8,128)(2,1)} %vc_hbm.1, ...), custom_call_target="tpu_custom_call" | custom-call | tf_op jit(solution)/shard_map/pallas_call | solution.py:479
  31.0 1.3 %copy.13 = bf16[1,8,1024]{2,1,0:T(8,128)(2,1)} copy(bf16[1,8,1024]{2,1,0:T(8,128)(2,1)} %shard_map.109) | data formatting | bytes 32768

commit v2 on v1

--- a/solution.py
+++ b/solution.py
@@ -152,12 +152,6 @@
     x_copy().start()
     for i in range(halves):
         wk_copy(i).start()
-    for i in range(halves):
-        wv_copy(i).start()
-    for i in range(pools):
-        kc_copy(i).start()
-    for i in range(pools):
-        vc_copy(i).start()
 
     def remote(kind, src, dst, peer):
         return pltpu.make_async_remote_copy(
@@ -248,12 +242,12 @@
     cos_v[...] = cosine
     sin_v[...] = sine
 
-    pl.semaphore_wait(barrier, ranks - 1)
     x_copy().wait()
 
     @pl.loop(0, halves)
     def _(i):
         wk_copy(i).wait()
+        wv_copy(i).start()
         product = jnp.dot(x_v[...], wk_v[i], preferred_element_type=jnp.float32)
         for j in range(2):
             h = pair_of(i) * 2 + j
@@ -269,12 +263,21 @@
                     scores[p * group : (p + 1) * group, p * page : (p + 1) * page] * scale
                 )
 
+        @pl.when(i == 0)
+        def _():
+            pl.semaphore_wait(barrier, ranks - 1)
+
+        for j in range(2):
+            h = pair_of(i) * 2 + j
+
             @pl.when(h != me)
             def _():
                 score_send(h).start()
 
-    for i in range(ranks):
-        ow_copy(i).start()
+    for i in range(pools):
+        kc_copy(i).start()
+    for i in range(pools):
+        vc_copy(i).start()
 
     @pl.loop(0, halves)
     def _(i):
@@ -301,6 +304,7 @@
     for d in range(1, ranks):
         weight_send(lax.rem(me + d, ranks)).start()
 
+
     for i in range(pools):
         kc_copy(i).wait()
     for i in range(pools):
@@ -309,6 +313,7 @@
 
     def resident(i, stats):
         h = head_of(i)
+        ow_copy(i).start()
         scores = (
             lax.dot_general(
                 q_all[h][:, :HD],

time: 32.5 us -> 31 us (0.954)
  Pallas kernels: 31 us -> 29.4 us
    pallas_call x1, Pallas kernels: 31 us -> 29.4 us  [fused(): pl.pallas_call(functools.partial(fused_kernel, ranks), out_shape=jax.Shap...]
where the time goes in v2:
time: 31 us; the launch traced here: 30.7 us
  Pallas kernels  29.4 us (95%)
  local copies, waits for them, and re-layouts  1.32 us (4%)
    pallas_call x1, Pallas kernels, fused(): pl.pallas_call(functools.partial(fused_kernel, ranks), out_shape=jax.Shap...  29.4 us
    unnamed x1, local copies, waits for them, and re-layouts  1.32 us

profile of v2, /device:TPU:0, one launch (start us, length us, event | category | flops | bytes accessed | tf_op | source)
XLA Modules:
  0.0 30.7 jit_solution(7892921553807854404)
XLA Ops:
  0.0 29.4 %shard_map.109 = bf16[1,8,1024]{2,1,0:T(8,128)(2,1)} custom-call(bf16[512,1024]{1,0:T(8,128)(2,1)} %x_hbm.1, bf16[1024,2048]{1,0:T(8,128)(2,1)} %w_hbm.1, s32[1,512]{1,0:T(1,128)} %seg_ref.1, s32[1,4]{1,0:T(1,128)} %dest_ref.1, s32[1,4]{1,0:T(1,128)} %slot_ref.1, bf16[1,8,8,128,128]{4,3,2,1,0:T(8,128)(2,1)} %kc_hbm.1, bf16[1,8,8,128,128]{4,3,2,1,0:T(8,128)(2,1)} %vc_hbm.1, ...), custom_call_target="tpu_custom_call" | custom-call | tf_op jit(solution)/shard_map/pallas_call | solution.py:484
  29.4 1.3 %copy.13 = bf16[1,8,1024]{2,1,0:T(8,128)(2,1)} copy(bf16[1,8,1024]{2,1,0:T(8,128)(2,1)} %shard_map.109) | data formatting | bytes 32768
